TPU v7x, 32 devices: a whole 2x2x4 slice. The times are simulated.
32 devices in a mesh: row: 8 (over y, x, core), col: 4 (over z).
Axes of the slice: x: 2, y: 2, z: 4, core: 2. Of those that a mesh axis runs over, the one named last changes fastest.
Arguments:
- in_map: bfloat16 [128, 128, 256], P('row', 'col'), may hold values from -6 to 6
- tile_w: bfloat16 [3, 3, 256, 256], replicated, may hold values from -0.125 to 0.125
- head_w1: bfloat16 [3, 3, 256, 256], replicated, may hold values from -0.125 to 0.125
- head_w2: bfloat16 [3, 3, 256, 256], replicated, may hold values from -0.125 to 0.125
- box_row: int32 [64, 4], P('row', 'col'), may hold values from 0 to 2
- box_col: int32 [64, 4], P('row', 'col'), may hold values from 0 to 18
- box_target: int32 [64, 4], P('row', 'col'), may hold values from -1 to 15, as said below
- head_cot: bfloat16 [32, 4, 14, 14, 256], P('row', 'col'), may hold values from -6 to 6
Outputs:
- grad_map: bfloat16 [128, 128, 256], P('row', 'col')
- grad_w1: float32 [3, 3, 256, 256], replicated
- grad_w2: float32 [3, 3, 256, 256], replicated
Inputs may be any that keep to these rules, and one draw needn't show every extreme that they name: `box_target`: within each row r of tiles, every head slot d * 4 + h (d below 4, h below 4) is named by exactly one tile slot, and empty slots hold -1. A tile names at most 2 head slots of one device, so it holds at most 8 boxes; in every row of tiles one tile holds 8 boxes, 2 for each device of the row.
All inputs are finite; a program needn't handle non-finite values.
Results may differ from a plain program's by a relative error of at most 0.012.
Values may be sent and summed in bfloat16 or wider, within the bound.
No kernel may reach another device: no remote copies, remote signals or barrier semaphores. Data moves between devices by JAX's collectives and lax.ppermute only.
A program may use at most 64 MiB of HBM per device.

v0:
```python
import math
import jax
import jax.numpy as jnp
from jax import lax
from jax.sharding import PartitionSpec as P

LAYOUT = ("NHWC", "HWIO", "NHWC")


def padded_2(shard, sides, width):
    for axis, dim in sides:
        size, length = (lax.axis_size(axis), shard.shape[dim])
        up = [(i, (i + 1) % size) for i in range(size - 1)]
        down = [(j, i) for i, j in up]
        last = lax.slice_in_dim(shard, length - width, length, axis=dim)
        leading = lax.slice_in_dim(shard, 0, width, axis=dim)
        before = lax.ppermute(last, axis, up)
        after = lax.ppermute(leading, axis, down)
        shard = jnp.concatenate([before, shard, after], axis=dim)
    return shard


def conv_pad(inputs, kernel, margin):
    return lax.conv_general_dilated(
        inputs,
        kernel,
        (1, 1),
        ((margin, margin), (margin, margin)),
        dimension_numbers=LAYOUT,
        preferred_element_type=jnp.float32,
    )


def flip_weights(kernel):
    return jnp.transpose(jnp.flip(kernel, (0, 1)), (0, 1, 3, 2))


def silu_slope(values):
    sigma = jax.nn.sigmoid(values)
    return sigma * (1.0 + values * (1.0 - sigma))


def weight_grad(inputs, deltas):
    channels = inputs.shape[-1]
    box_side = inputs.shape[1]
    padded = jnp.pad(inputs, ((0, 0), (1, 1), (1, 1), (0, 0)))
    flat_delta = deltas.reshape(-1, channels)
    blocks = []
    for shift_y in range(3):
        for shift_x in range(3):
            window = padded[
                :, shift_y : shift_y + box_side, shift_x : shift_x + box_side, :
            ].reshape(-1, channels)
            blocks.append(
                lax.dot_general(
                    window, flat_delta, (((0,), (0,)), ((), ())), preferred_element_type=jnp.float32
                )
            )
    return jnp.stack(blocks).reshape(3, 3, channels, channels)


def pick_rows(table, values):
    flat = values.reshape(values.shape[0], -1)
    return jnp.dot(table, flat, preferred_element_type=jnp.float32).astype(jnp.bfloat16)


def pick_back(table, values):
    return lax.dot_general(
        table, values, (((0,), (0,)), ((), ())), preferred_element_type=jnp.float32
    ).astype(jnp.bfloat16)


def body(in_map, tile_w, head_w1, head_w2, box_row, box_col, box_target, head_cot):
    tile_rows, tile_cols, channels = in_map.shape
    head_count = head_cot.shape[0]
    box_side = head_cot.shape[2]
    slot_count = box_target.shape[0]
    columns = lax.axis_size("col")
    capacity = slot_count // columns
    pair_count = columns * capacity
    padded = padded_2(in_map, (("row", 0), ("col", 1)), 1)
    preact = conv_pad(padded[None], tile_w, 0)[0]
    target = box_target[:, 0]
    occupied = target >= 0
    dest_col = jnp.where(occupied, target // head_count, 0)
    head_slot = jnp.where(occupied, target % head_count, 0)
    slot_ids = jnp.arange(slot_count, dtype=jnp.int32)
    same_dest = (dest_col[:, None] == dest_col[None, :]) & occupied[None, :]
    placing = jnp.sum(same_dest & (slot_ids[None, :] < slot_ids[:, None]), axis=1)
    pair_slot = dest_col * capacity + placing
    pair_ids = jnp.arange(pair_count, dtype=jnp.int32)
    send_map = ((pair_slot[None, :] == pair_ids[:, None]) & occupied[None, :]).astype(jnp.bfloat16)
    head_ids = jnp.arange(head_count, dtype=jnp.int32)
    head_hot = ((head_slot[:, None] == head_ids[None, :]) & occupied[:, None]).astype(jnp.bfloat16)
    pair_head = (
        jnp.dot(send_map, head_hot, preferred_element_type=jnp.float32)
        .astype(jnp.bfloat16)
        .reshape(columns, capacity, head_count)
    )
    top_row = box_row[:, 0]
    left_col = box_col[:, 0]
    zero_index = jnp.zeros((), jnp.int32)
    window = box_side + 2
    windows = jax.vmap(
        lambda y, x: lax.dynamic_slice(padded, (y, x, zero_index), (window, window, channels))
    )(top_row, left_col)
    outgoing = pick_rows(send_map, windows).reshape(columns, capacity, window, window, channels)
    arrived, arrived_head = (
        lax.all_to_all(outgoing, "col", split_axis=0, concat_axis=0, tiled=True),
        lax.all_to_all(pair_head, "col", split_axis=0, concat_axis=0, tiled=True),
    )
    arrived_head = arrived_head.reshape(pair_count, head_count)
    gathered = pick_back(arrived_head, arrived.reshape(pair_count, -1)).reshape(
        head_count, window, window, channels
    )
    box_input = jax.nn.silu(conv_pad(gathered, tile_w, 0)).astype(jnp.bfloat16)
    factor = 1.0 / math.sqrt(lax.axis_size("row") * columns * head_count * box_side * box_side)
    cotangent = head_cot[:, 0]
    pre_one = conv_pad(box_input, head_w1, 1)
    hidden = jax.nn.silu(pre_one).astype(jnp.bfloat16)
    pre_two = conv_pad(hidden, head_w2, 1)
    delta_two = (cotangent.astype(jnp.float32) * silu_slope(pre_two)).astype(jnp.bfloat16)
    second_local = weight_grad(hidden, delta_two)
    delta_one = (conv_pad(delta_two, flip_weights(head_w2), 1) * silu_slope(pre_one)).astype(
        jnp.bfloat16
    )
    box_grads = conv_pad(delta_one, flip_weights(head_w1), 1).astype(jnp.bfloat16)
    sent_back = pick_rows(arrived_head, box_grads).reshape(
        columns, capacity, box_side, box_side, channels
    )
    returned = lax.all_to_all(sent_back, "col", split_axis=0, concat_axis=0, tiled=True)
    slot_grads = pick_back(send_map, returned.reshape(pair_count, -1)).reshape(
        slot_count, box_side, box_side, channels
    )
    first_local = weight_grad(box_input, delta_one)
    first_sum, second_sum = lax.psum((first_local, second_local), ("row", "col"))

    def add_box(slot, running):
        current = lax.dynamic_slice(
            running, (top_row[slot], left_col[slot], zero_index), (box_side, box_side, channels)
        )
        return lax.dynamic_update_slice(
            running,
            current + slot_grads[slot].astype(jnp.float32),
            (top_row[slot], left_col[slot], zero_index),
        )

    box_total = lax.fori_loop(
        0, slot_count, add_box, jnp.zeros((tile_rows, tile_cols, channels), jnp.float32)
    )
    delta_map = (box_total * silu_slope(preact)).astype(jnp.bfloat16)
    delta_rim = padded_2(delta_map, (("row", 0), ("col", 1)), 1)
    grad_map = conv_pad(delta_rim[None], flip_weights(tile_w), 0)[0].astype(jnp.bfloat16)
    return (grad_map, first_sum * factor, second_sum * factor)


def solution(mesh):
    in_specs = (
        P("row", "col", None),
        P(),
        P(),
        P(),
        P("row", "col"),
        P("row", "col"),
        P("row", "col"),
        P("row", "col", None, None, None),
    )
    out_specs = (P("row", "col", None), P(), P())
    return jax.shard_map(body, mesh=mesh, in_specs=in_specs, out_specs=out_specs, check_vma=False)
```

profile of v0, /device:TPU:0, one launch (start us, length us, event | category | flops | bytes accessed | tf_op | source)
XLA Modules:
  0.0 296.8 jit_solution(2329614647910186350)
XLA Ops:
  9.3 3.0 %collective-permute-start = (bf16[1,32,256]{2,1,0:T(8,128)(2,1)S(1)}, bf16[1,32,256]{2,1,0:T(8,128)(2,1)S(1)}, u32[]{:S(2)}, u32[]{:S(2)}) collective-permute-start(bf16[1,32,256]{2,1,0:T(8,128)(2,1)S(1)} %get-tuple-element.174), channel_id=1, source_target_pairs={{0,4},{4,8},{8,12},{12,16},{16,20},{20,24},{24,28},{1,5},{5,9},{9,... | collective-permute-start | bytes 49160 | tf_op jit(solution)/shard_map/ppermute | solution.py:17
  16.9 5.0 %collective-permute-start.2 = (bf16[18,1,256]{2,1,0:T(2,128)(2,1)S(1)}, bf16[18,1,256]{2,1,0:T(2,128)(2,1)S(1)}, u32[]{:S(2)}, u32[]{:S(2)}) collective-permute-start(bf16[18,1,256]{2,1,0:T(2,128)(2,1)S(1)} %get-tuple-element.169), channel_id=1, source_target_pairs={{0,1},{1,2},{2,3},{4,5},{5,6},{6,7},{8,9},{9,10},{10,11},{12,13},{... | collective-permute-start | bytes 27656 | tf_op jit(solution)/shard_map/ppermute | solution.py:17
  23.3 4.3 %collective-permute-done.3 = bf16[18,1,256]{2,1,0:T(2,128)(2,1)S(1)} collective-permute-done((bf16[18,1,256]{2,1,0:T(2,128)(2,1)S(1)}, bf16[18,1,256]{2,1,0:T(2,128)(2,1)S(1)}, u32[]{:S(2)}, u32[]{:S(2)}) %collective-permute-start.3) | collective-permute-done | bytes 9248 | tf_op jit(solution)/shard_map/ppermute | solution.py:18
  27.8 20.0 %while.15 = (s32[]{:T(128)}, bf16[18,34,256]{2,1,0:T(8,128)(2,1)S(1)}, s32[8,3]{0,1:T(4,128)S(1)}, bf16[8,16,16,256]{3,2,1,0:T(8,128)(2,1)}, s32[]{:T(128)}) while((s32[]{:T(128)}, bf16[18,34,256]{2,1,0:T(8,128)(2,1)S(1)}, s32[8,3]{0,1:T(4,128)S(1)}, bf16[8,16,16,256]{3,2,1,0:T(8,128)(2,1)}, s32[]{:T(128)}) %tuple.64), condition=%wide.while_cond, body=%wide.while_body.sunk | while | flops 2 | bytes 263285 | solution.py:105
  28.4 1.9 bitcast_dynamic-update-slice_fusion.2
  30.9 1.9 bitcast_dynamic-update-slice_fusion.2
  33.4 1.9 bitcast_dynamic-update-slice_fusion.2
  35.9 1.9 bitcast_dynamic-update-slice_fusion.2
  38.4 1.9 bitcast_dynamic-update-slice_fusion.2
  40.9 1.9 bitcast_dynamic-update-slice_fusion.2
  45.9 1.9 bitcast_dynamic-update-slice_fusion.2
  51.2 4.0 %all-to-all-start.1 = ((bf16[4,2,16,16,256]{4,3,2,1,0:T(8,128)(2,1)}), bf16[4,2,16,16,256]{4,3,2,1,0:T(8,128)(2,1)S(1)}, u32[]{:S(2)}, u32[]{:S(2)}) async-start(bf16[4,2,16,16,256]{4,3,2,1,0:T(8,128)(2,1)} %bitcast.140), calls=%async_computation.1 | async-start | bytes 2097152 | tf_op jit(solution)/shard_map/all_to_all | solution.py:109
  58.4 22.7 %all-to-all-done.1 = bf16[4,2,16,16,256]{4,3,2,1,0:T(8,128)(2,1)S(1)} async-done(((bf16[4,2,16,16,256]{4,3,2,1,0:T(8,128)(2,1)}), bf16[4,2,16,16,256]{4,3,2,1,0:T(8,128)(2,1)S(1)}, u32[]{:S(2)}, u32[]{:S(2)}) %all-to-all-start.1) | async-done | bytes 1048608 | tf_op jit(solution)/shard_map/all_to_all | solution.py:109
  81.0 3.4 %all-to-all-start = ((bf16[4,2,4]{2,1,0:T(2,128)(2,1)}), bf16[4,2,4]{2,1,0:T(2,128)(2,1)S(1)}, u32[]{:S(2)}, u32[]{:S(2)}) async-start(bf16[4,2,4]{2,1,0:T(2,128)(2,1)} %bitcast.9), calls=%async_computation | async-start | bytes 4096 | tf_op jit(solution)/shard_map/all_to_all | solution.py:110
  84.9 4.8 %all-to-all-done = bf16[4,2,4]{2,1,0:T(2,128)(2,1)S(1)} async-done(((bf16[4,2,4]{2,1,0:T(2,128)(2,1)}), bf16[4,2,4]{2,1,0:T(2,128)(2,1)S(1)}, u32[]{:S(2)}, u32[]{:S(2)}) %all-to-all-start) | async-done | bytes 96 | tf_op jit(solution)/shard_map/all_to_all | solution.py:110
  101.6 2.9 fusion.9
  106.2 2.3 copy.120
  111.4 2.5 convolution_convert_fusion.4
  118.1 3.5 %all-to-all-start.2 = ((bf16[4,2,14,14,256]{4,1,3,2,0:T(2,128)(2,1)}), bf16[4,2,14,14,256]{4,1,3,2,0:T(2,128)(2,1)S(1)}, u32[]{:S(2)}, u32[]{:S(2)}) async-start(bf16[4,2,14,14,256]{4,1,3,2,0:T(2,128)(2,1)} %copy.105), calls=%async_computation.2 | async-start | bytes 1605632 | tf_op jit(solution)/shard_map/all_to_all | solution.py:131
  141.9 45.4 %while.14 = (s32[]{:T(128)}, f32[16,32,256]{2,0,1:T(8,128)S(1)}, s32[8]{0:T(128)S(1)}, s32[8]{0:T(128)S(1)}, bf16[8,14,14,256]{3,2,1,0:T(8,128)(2,1)S(1)}, /*index=5*/s32[]{:T(128)}, s32[]{:T(128)}, s32[]{:T(128)}, s32[]{:T(128)}) while((s32[]{:T(128)}, f32[16,32,256]{2,0,1:T(8,128)S(1)}, s32[8]{0:T(128)S(1)}, s32[8]{0:T(128)S(1)}, ...), condition=%wide.region_2.3_spmd, body=%wide.region_1.2_spmd.sunk | while | flops 100360 | bytes 1706193 | solution.py:148
  190.2 4.3 %collective-permute-done.5 = bf16[1,32,256]{2,0,1:T(2,128)(2,1)S(1)} collective-permute-done((bf16[1,32,256]{2,0,1:T(2,128)(2,1)S(1)}, bf16[1,32,256]{2,0,1:T(2,128)(2,1)S(1)}, u32[]{:S(2)}, u32[]{:S(2)}) %collective-permute-start.5) | collective-permute-done | bytes 16416 | tf_op jit(solution)/shard_map/ppermute | solution.py:18
  197.8 4.2 %collective-permute-done.7 = bf16[18,1,256]{2,0,1:T(8,128)(2,1)S(1)} collective-permute-done((bf16[18,1,256]{2,0,1:T(8,128)(2,1)S(1)}, bf16[18,1,256]{2,0,1:T(8,128)(2,1)S(1)}, u32[]{:S(2)}, u32[]{:S(2)}) %collective-permute-start.7) | collective-permute-done | bytes 9248 | tf_op jit(solution)/shard_map/ppermute | solution.py:18
  204.3 80.6 %all-reduce.5.cloned.1.call-done = (f32[3,3,256,256]{3,2,1,0:T(8,128)}, f32[3,3,256,256]{3,2,1,0:T(8,128)}) async-done(((f32[3,3,256,256]{3,2,1,0:T(8,128)}, f32[3,3,256,256]{3,2,1,0:T(8,128)}), (f32[3,3,256,256]{3,2,1,0:T(8,128)}, f32[3,3,256,256]{3,2,1,0:T(8,128)})) %all-reduce.5.cloned.1.call-update) | async-done | bytes 4718608 | tf_op jit(solution)/shard_map/psum | solution.py:136
  284.9 3.4 %broadcast_multiply_fusion.1 = f32[3,3,256,256]{3,2,1,0:T(8,128)} fusion(f32[3,3,256,256]{3,2,1,0:T(8,128)} %get-tuple-element.153), kind=kLoop, calls=%fused_computation.29 | loop fusion | flops 589824 | bytes 4718592 | tf_op jit(solution)/shard_map/mul | solution.py:154
  (220 shorter events, 86.3 us)
Async XLA Ops:
  7.2 49.2 %copy-start = (bf16[3,3,256,256]{3,2,1,0:T(8,128)(2,1)S(1)}, bf16[3,3,256,256]{3,2,1,0:T(8,128)(2,1)}, u32[]{:S(2)}) copy-start(bf16[3,3,256,256]{3,2,1,0:T(8,128)(2,1)} %param.11) | copy-start | bytes 3538948
  8.0 8.8 %collective-permute-start.1 = (bf16[1,32,256]{2,1,0:T(8,128)(2,1)S(1)}, bf16[1,32,256]{2,1,0:T(8,128)(2,1)S(1)}, u32[]{:S(2)}, u32[]{:S(2)}) collective-permute-start(bf16[1,32,256]{2,1,0:T(8,128)(2,1)S(1)} %get-tuple-element.173), channel_id=1, source_target_pairs={{4,0},{8,4},{12,8},{16,12},{20,16},{24,20},{28,24},{5,1},{9,5},{13... | collective-permute-start | bytes 49160 | tf_op jit(solution)/shard_map/ppermute | solution.py:18
  9.3 6.6 %collective-permute-start = (bf16[1,32,256]{2,1,0:T(8,128)(2,1)S(1)}, bf16[1,32,256]{2,1,0:T(8,128)(2,1)S(1)}, u32[]{:S(2)}, u32[]{:S(2)}) collective-permute-start(bf16[1,32,256]{2,1,0:T(8,128)(2,1)S(1)} %get-tuple-element.174), channel_id=1, source_target_pairs={{0,4},{4,8},{8,12},{12,16},{16,20},{20,24},{24,28},{1,5},{5,9},{9,... | collective-permute-start | bytes 49160 | tf_op jit(solution)/shard_map/ppermute | solution.py:17
  16.9 6.4 %collective-permute-start.2 = (bf16[18,1,256]{2,1,0:T(2,128)(2,1)S(1)}, bf16[18,1,256]{2,1,0:T(2,128)(2,1)S(1)}, u32[]{:S(2)}, u32[]{:S(2)}) collective-permute-start(bf16[18,1,256]{2,1,0:T(2,128)(2,1)S(1)} %get-tuple-element.169), channel_id=1, source_target_pairs={{0,1},{1,2},{2,3},{4,5},{5,6},{6,7},{8,9},{9,10},{10,11},{12,13},{... | collective-permute-start | bytes 27656 | tf_op jit(solution)/shard_map/ppermute | solution.py:17
  21.9 5.7 %collective-permute-start.3 = (bf16[18,1,256]{2,1,0:T(2,128)(2,1)S(1)}, bf16[18,1,256]{2,1,0:T(2,128)(2,1)S(1)}, u32[]{:S(2)}, u32[]{:S(2)}) collective-permute-start(bf16[18,1,256]{2,1,0:T(2,128)(2,1)S(1)} %get-tuple-element.170), channel_id=1, source_target_pairs={{1,0},{2,1},{3,2},{5,4},{6,5},{7,6},{9,8},{10,9},{11,10},{13,12},{... | collective-permute-start | bytes 27656 | tf_op jit(solution)/shard_map/ppermute | solution.py:18
  50.0 5.2 %copy-start.19 = (s32[8,1]{0,1:T(1,128)S(1)}, s32[8,1]{0,1:T(1,128)}, u32[]{:S(2)}) copy-start(s32[8,1]{0,1:T(1,128)} %param.16) | copy-start | bytes 100
  51.2 5.2 %copy-start.20 = (pred[8,5]{0,1:T(8,128)(4,1)S(1)}, pred[8,5]{0,1:T(8,128)(4,1)}, u32[]{:S(2)}) copy-start(pred[8,5]{0,1:T(8,128)(4,1)} %constant.129) | copy-start | bytes 124
  51.2 29.9 %all-to-all-start.1 = ((bf16[4,2,16,16,256]{4,3,2,1,0:T(8,128)(2,1)}), bf16[4,2,16,16,256]{4,3,2,1,0:T(8,128)(2,1)S(1)}, u32[]{:S(2)}, u32[]{:S(2)}) async-start(bf16[4,2,16,16,256]{4,3,2,1,0:T(8,128)(2,1)} %bitcast.140), calls=%async_computation.1 | async-start | bytes 2097152 | tf_op jit(solution)/shard_map/all_to_all | solution.py:109
  81.0 8.7 %all-to-all-start = ((bf16[4,2,4]{2,1,0:T(2,128)(2,1)}), bf16[4,2,4]{2,1,0:T(2,128)(2,1)S(1)}, u32[]{:S(2)}, u32[]{:S(2)}) async-start(bf16[4,2,4]{2,1,0:T(2,128)(2,1)} %bitcast.9), calls=%async_computation | async-start | bytes 4096 | tf_op jit(solution)/shard_map/all_to_all | solution.py:110
  94.7 1.8 copy-start.17
  105.3 6.1 %copy-start.4 = (bf16[14,4,16,256]{3,2,1,0:T(8,128)(2,1)}, bf16[14,4,16,256]{3,2,1,0:T(8,128)(2,1)S(1)}, u32[]{:S(2)}) copy-start(bf16[14,4,16,256]{3,2,1,0:T(8,128)(2,1)S(1)} %reshape.159) | copy-start | bytes 1376260
  116.3 5.3 %copy-start.10 = (bf16[4,14,14,256]{3,2,1,0:T(8,128)(2,1)S(1)}, bf16[4,14,14,256]{3,2,1,0:T(8,128)(2,1)}, u32[]{:S(2)}) copy-start(bf16[4,14,14,256]{3,2,1,0:T(8,128)(2,1)} %copy_bitcast_fusion.2) | copy-start | bytes 1204228
  118.1 22.3 %all-to-all-start.2 = ((bf16[4,2,14,14,256]{4,1,3,2,0:T(2,128)(2,1)}), bf16[4,2,14,14,256]{4,1,3,2,0:T(2,128)(2,1)S(1)}, u32[]{:S(2)}, u32[]{:S(2)}) async-start(bf16[4,2,14,14,256]{4,1,3,2,0:T(2,128)(2,1)} %copy.105), calls=%async_computation.2 | async-start | bytes 1605632 | tf_op jit(solution)/shard_map/all_to_all | solution.py:131
  121.6 1.5 copy-start.12
  121.6 163.3 %all-reduce.5.cloned.1.call-start = ((), (), s32[]{:S(2)}) async-start(), calls=%async_computation.3 | async-start | bytes 9437184 | tf_op jit(solution)/shard_map/psum | solution.py:136
  134.0 1.5 copy-start.2
  140.6 1.3 copy-start.15
  140.6 1.3 copy-start.16
  141.9 45.5 %copy-start.3 = (f32[16,8,5,256]{3,0,2,1:T(8,128)S(1)}, f32[16,8,5,256]{3,0,2,1:T(8,128)}, u32[]{:S(2)}) copy-start(f32[16,8,5,256]{3,0,2,1:T(8,128)} %copy.111) | copy-start | bytes 1966084
  187.6 2.6 collective-permute-start.4
  188.9 5.6 %collective-permute-start.5 = (bf16[1,32,256]{2,0,1:T(2,128)(2,1)S(1)}, bf16[1,32,256]{2,0,1:T(2,128)(2,1)S(1)}, u32[]{:S(2)}, u32[]{:S(2)}) collective-permute-start(bf16[1,32,256]{2,0,1:T(2,128)(2,1)S(1)} %get-tuple-element.172), channel_id=1, source_target_pairs={{4,0},{8,4},{12,8},{16,12},{20,16},{24,20},{28,24},{5,1},{9,5},{13... | collective-permute-start | bytes 49160 | tf_op jit(solution)/shard_map/ppermute | solution.py:18
  194.6 3.2 %collective-permute-start.6 = (bf16[18,1,256]{2,0,1:T(8,128)(2,1)S(1)}, bf16[18,1,256]{2,0,1:T(8,128)(2,1)S(1)}, u32[]{:S(2)}, u32[]{:S(2)}) collective-permute-start(bf16[18,1,256]{2,0,1:T(8,128)(2,1)S(1)} %get-tuple-element.167), channel_id=1, source_target_pairs={{0,1},{1,2},{2,3},{4,5},{5,6},{6,7},{8,9},{9,10},{10,11},{12,13},{... | collective-permute-start | bytes 27656 | tf_op jit(solution)/shard_map/ppermute | solution.py:17
  196.4 5.6 %collective-permute-start.7 = (bf16[18,1,256]{2,0,1:T(8,128)(2,1)S(1)}, bf16[18,1,256]{2,0,1:T(8,128)(2,1)S(1)}, u32[]{:S(2)}, u32[]{:S(2)}) collective-permute-start(bf16[18,1,256]{2,0,1:T(8,128)(2,1)S(1)} %get-tuple-element.168), channel_id=1, source_target_pairs={{1,0},{2,1},{3,2},{5,4},{6,5},{7,6},{9,8},{10,9},{11,10},{13,12},{... | collective-permute-start | bytes 27656 | tf_op jit(solution)/shard_map/ppermute | solution.py:18
  284.9 3.4 %copy-start.1 = (f32[3,3,256,256]{3,2,1,0:T(8,128)S(1)}, f32[3,3,256,256]{3,2,1,0:T(8,128)}, u32[]{:S(2)}) copy-start(f32[3,3,256,256]{3,2,1,0:T(8,128)} %get-tuple-element.154) | copy-start | bytes 7077892
  (9 other events, 9.2 us)
Sparse Core Ops, SparseCore 0:
  138.8 146.0 all-reduce.4
where the time goes:
time: 298 us; the launch traced here: 297 us
  waiting for transfers between devices  123 us (41%)
  local copies, waits for them, and re-layouts  60.4 us (20%)
  loops' own time  31.5 us (11%)
  starting transfers between devices  27.2 us (9%)
  matrix products  27.2 us (9%)
  between operations  14.9 us (5%)
  other arithmetic  12.8 us (4%)
    psum x1, waiting for transfers between devices, body(): lax.psum((first_local, second_local), ('row', 'col'))  80.6 us
    another operation x1, loops' own time, body(): lax.fori_loop(0, slot_count, add_box, jnp.zeros((tile_rows, tile_cols, ch...  31.5 us
    all_to_all x1, waiting for transfers between devices, body(): lax.all_to_all(outgoing, 'col', split_axis=0, concat_axis=0, tiled=True)  22.7 us
    gather x24, local copies, waits for them, and re-layouts  19.9 us
    dot_general x18, matrix products, weight_grad(): lax.dot_general(window, flat_delta, (((0,), (0,)), ((), ())), preferred_e...  14 us
    ppermute x4, waiting for transfers between devices, padded_2(): after = lax.ppermute(leading, axis, down)  12.8 us
    ppermute x4, starting transfers between devices, padded_2(): before = lax.ppermute(last, axis, up)  11.1 us
    conv_general_dilated x7, matrix products, conv_pad(): lax.conv_general_dilated(inputs, kernel, (1, 1), ((margin, margin), (marg...  11.1 us
  transfers between devices with their start and end apart: 12, of which 9 were waited for; matrix products, arithmetic and copies ran while one was open for 13% of the time, Pallas kernels for 0%

commit v1 on v0

--- a/solution.py
+++ b/solution.py
@@ -5,6 +5,29 @@
 from jax.sharding import PartitionSpec as P
 
 LAYOUT = ("NHWC", "HWIO", "NHWC")
+
+
+def cut_along(value, dim, size):
+    shape = value.shape
+    pieces = value.reshape(*shape[:dim], size, shape[dim] // size, *shape[dim + 1 :])
+    return jnp.moveaxis(pieces, dim, 0)
+
+
+def joined_along(blocks, dim):
+    shape = list(blocks.shape[1:])
+    shape[dim] *= blocks.shape[0]
+    return jnp.moveaxis(blocks, 0, dim).reshape(shape)
+
+
+def exchange_directly(x, axis, split_dim, concat_dim):
+    count, index = (lax.axis_size(axis), lax.axis_index(axis))
+    tiles = cut_along(x, split_dim, count)
+    outs = [tiles[index]]
+    for step in range(1, count):
+        sent = tiles[(index + step) % count]
+        outs.append(lax.ppermute(sent, axis, [(i, (i + step) % count) for i in range(count)]))
+    tiles = jnp.stack(outs)[(index - jnp.arange(count)) % count]
+    return joined_along(tiles, concat_dim)
 
 
 def padded_2(shard, sides, width):
@@ -106,7 +129,7 @@
     )(top_row, left_col)
     outgoing = pick_rows(send_map, windows).reshape(columns, capacity, window, window, channels)
     arrived, arrived_head = (
-        lax.all_to_all(outgoing, "col", split_axis=0, concat_axis=0, tiled=True),
+        exchange_directly(outgoing, "col", 0, 0),
         lax.all_to_all(pair_head, "col", split_axis=0, concat_axis=0, tiled=True),
     )
     arrived_head = arrived_head.reshape(pair_count, head_count)

time: 298 us -> 288 us (0.966)
  waiting for transfers between devices: 123 us -> 115 us
  local copies, waits for them, and re-layouts: 60.4 us -> 54.4 us
    all_to_all x1 -> x0, waiting for transfers between devices: 22.7 us -> none  [body(): lax.all_to_all(outgoing, 'col', split_axis=0, concat_axis=0, tiled=True)]
    ppermute x0 -> x3, waiting for transfers between devices: none -> 19.6 us  [exchange_directly(): lax.ppermute(sent, axis, [(i, (i + step) % count) for i in range(count)])]
    all_to_all x1, waiting for transfers between devices: 4.8 us -> 0.01 us  [body(): lax.all_to_all(pair_head, 'col', split_axis=0, concat_axis=0, tiled=True)]
    ppermute x0 -> x3, starting transfers between devices: none -> 4.44 us  [exchange_directly(): lax.ppermute(sent, axis, [(i, (i + step) % count) for i in range(count)])]
    all_to_all x1 -> x0, starting transfers between devices: 3.99 us -> none  [body(): lax.all_to_all(outgoing, 'col', split_axis=0, concat_axis=0, tiled=True)]
    gather x24 -> x25, local copies, waits for them, and re-layouts: 19.9 us -> 16.2 us
    unnamed x49 -> x47, local copies, waits for them, and re-layouts: 9.91 us -> 7.71 us
  transfers between devices with their start and end apart: 12 -> 14, of which waited for: 9 -> 9; matrix products, arithmetic and copies ran while one was open for 13% -> 19% of each run, Pallas kernels for 0% -> 0%
where the time goes in v1:
time: 288 us; the launch traced here: 286 us
  waiting for transfers between devices  115 us (40%)
  local copies, waits for them, and re-layouts  54.4 us (19%)
  loops' own time  31.7 us (11%)
  starting transfers between devices  29 us (10%)
  matrix products  27.2 us (9%)
  between operations  14.9 us (5%)
  other arithmetic  13.7 us (5%)
    psum x1, waiting for transfers between devices, body(): lax.psum((first_local, second_local), ('row', 'col'))  79.8 us
    another operation x1, loops' own time, body(): lax.fori_loop(0, slot_count, add_box, jnp.zeros((tile_rows, tile_cols, ch...  31.5 us
    ppermute x3, waiting for transfers between devices, exchange_directly(): lax.ppermute(sent, axis, [(i, (i + step) % count) for i in range(count)])  19.6 us
    gather x24, local copies, waits for them, and re-layouts  15.6 us
    dot_general x18, matrix products, weight_grad(): lax.dot_general(window, flat_delta, (((0,), (0,)), ((), ())), preferred_e...  14 us
    ppermute x4, waiting for transfers between devices, padded_2(): after = lax.ppermute(leading, axis, down)  12.4 us
    conv_general_dilated x7, matrix products, conv_pad(): lax.conv_general_dilated(inputs, kernel, (1, 1), ((margin, margin), (marg...  11.3 us
    ppermute x4, starting transfers between devices, padded_2(): before = lax.ppermute(last, axis, up)  9.54 us
  transfers between devices with their start and end apart: 14, of which 9 were waited for; matrix products, arithmetic and copies ran while one was open for 19% of the time, Pallas kernels for 0%

profile of v1, /device:TPU:0, one launch (start us, length us, event | category | flops | bytes accessed | tf_op | source)
XLA Modules:
  0.0 286.0 jit_solution(11104835893836966281)
XLA Ops:
  11.7 6.3 %all-to-all-start = ((bf16[4,2,4]{2,1,0:T(2,128)(2,1)}), bf16[4,2,4]{2,1,0:T(2,128)(2,1)S(1)}, u32[]{:S(2)}, u32[]{:S(2)}) async-start(bf16[4,2,4]{2,1,0:T(2,128)(2,1)} %bitcast.9), calls=%async_computation | async-start | bytes 4096 | tf_op jit(solution)/shard_map/all_to_all | solution.py:133
  20.1 3.0 %collective-permute-start = (bf16[1,32,256]{2,1,0:T(8,128)(2,1)S(1)}, bf16[1,32,256]{2,1,0:T(8,128)(2,1)S(1)}, u32[]{:S(2)}, u32[]{:S(2)}) collective-permute-start(bf16[1,32,256]{2,1,0:T(8,128)(2,1)S(1)} %get-tuple-element.178), channel_id=1, source_target_pairs={{0,4},{4,8},{8,12},{12,16},{16,20},{20,24},{24,28},{1,5},{5,9},{9,... | collective-permute-start | bytes 49160 | tf_op jit(solution)/shard_map/ppermute | solution.py:40
  25.0 3.9 %collective-permute-start.2 = (bf16[18,1,256]{2,1,0:T(2,128)(2,1)S(1)}, bf16[18,1,256]{2,1,0:T(2,128)(2,1)S(1)}, u32[]{:S(2)}, u32[]{:S(2)}) collective-permute-start(bf16[18,1,256]{2,1,0:T(2,128)(2,1)S(1)} %get-tuple-element.173), channel_id=1, source_target_pairs={{0,1},{1,2},{2,3},{4,5},{5,6},{6,7},{8,9},{9,10},{10,11},{12,13},{... | collective-permute-start | bytes 27656 | tf_op jit(solution)/shard_map/ppermute | solution.py:40
  30.4 4.3 %collective-permute-done.3 = bf16[18,1,256]{2,1,0:T(2,128)(2,1)S(1)} collective-permute-done((bf16[18,1,256]{2,1,0:T(2,128)(2,1)S(1)}, bf16[18,1,256]{2,1,0:T(2,128)(2,1)S(1)}, u32[]{:S(2)}, u32[]{:S(2)}) %collective-permute-start.3) | collective-permute-done | bytes 9248 | tf_op jit(solution)/shard_map/ppermute | solution.py:41
  35.1 15.8 %while.15 = (s32[]{:T(128)}, bf16[18,34,256]{2,1,0:T(8,128)(2,1)S(1)}, s32[8,3]{0,1:T(4,128)S(1)}, bf16[8,16,16,256]{3,2,1,0:T(8,128)(2,1)S(1)}, s32[]{:T(128)}) while((s32[]{:T(128)}, bf16[18,34,256]{2,1,0:T(8,128)(2,1)S(1)}, s32[8,3]{0,1:T(4,128)S(1)}, bf16[8,16,16,256]{3,2,1,0:T(8,128)(2,1)S(1)}, s32[]{:T(128)}) %tuple.67), condition=%wide.while_cond, body=%wide.while_body.sunk | while | flops 2 | bytes 262269 | solution.py:128
  35.7 1.3 bitcast_dynamic-update-slice_fusion.2
  52.2 1.5 collective-permute-start.6
  53.7 1.5 collective-permute-start.5
  55.2 1.5 collective-permute-start.4
  58.7 1.9 collective-permute-done.6
  60.5 17.7 %collective-permute-done.5 = bf16[1,2,16,16,256]{4,3,2,1,0:T(8,128)(2,1)S(1)} collective-permute-done((bf16[1,2,16,16,256]{4,3,2,1,0:T(8,128)(2,1)S(1)}, bf16[1,2,16,16,256]{4,3,2,1,0:T(8,128)(2,1)S(1)}, u32[]{:S(2)}, u32[]{:S(2)}) %collective-permute-start.5) | collective-permute-done | bytes 262176 | tf_op jit(solution)/shard_map/ppermute | solution.py:28
  91.4 2.9 %fusion.9 = bf16[14,32,2,256]{3,1,2,0:T(8,128)(2,1)S(1)} fusion(bf16[3,3,256,256]{3,2,1,0:T(8,128)(2,1)} %param.13, bf16[14,4,7,2,256]{4,2,1,3,0:T(8,128)(2,1)S(1)} %slice.140, bf16[14,4,8,2,256]{4,2,1,3,0:T(8,128)(2,1)S(1)} %copy.102, f32[14,32,2,256]{3,1,2,0:T(8,128)} %copy-done.8, pred[32,2]{0,1:T(4,128)(4,1)S(1)} %copy-done.14), kind=kOutput, calls=%fused_computation.24 | convolution fusion | flops 1011679232 | bytes 3416128 | tf_op jit(solution)/shard_map/conv_general_dilated | solution.py:47
  95.9 2.3 copy.120
  101.2 2.8 convolution_convert_fusion.4
  106.1 1.8 copy.105
  107.8 3.5 %all-to-all-start.1 = ((bf16[4,2,14,14,256]{4,1,3,2,0:T(2,128)(2,1)}), bf16[4,2,14,14,256]{4,1,3,2,0:T(2,128)(2,1)S(1)}, u32[]{:S(2)}, u32[]{:S(2)}) async-start(bf16[4,2,14,14,256]{4,1,3,2,0:T(2,128)(2,1)} %copy.105), calls=%async_computation.1 | async-start | bytes 1605632 | tf_op jit(solution)/shard_map/all_to_all | solution.py:154
  111.4 1.4 fusion.28
  128.4 3.0 %all-to-all-done.1 = bf16[4,2,14,14,256]{4,1,3,2,0:T(2,128)(2,1)S(1)} async-done(((bf16[4,2,14,14,256]{4,1,3,2,0:T(2,128)(2,1)}), bf16[4,2,14,14,256]{4,1,3,2,0:T(2,128)(2,1)S(1)}, u32[]{:S(2)}, u32[]{:S(2)}) %all-to-all-start.1) | async-done | bytes 802848 | tf_op jit(solution)/shard_map/all_to_all | solution.py:154
  132.8 45.5 %while.14 = (s32[]{:T(128)}, f32[16,32,256]{2,0,1:T(8,128)S(1)}, s32[8]{0:T(128)S(1)}, s32[8]{0:T(128)S(1)}, bf16[8,14,14,256]{3,2,1,0:T(8,128)(2,1)S(1)}, /*index=5*/s32[]{:T(128)}, s32[]{:T(128)}, s32[]{:T(128)}, s32[]{:T(128)}) while((s32[]{:T(128)}, f32[16,32,256]{2,0,1:T(8,128)S(1)}, s32[8]{0:T(128)S(1)}, s32[8]{0:T(128)S(1)}, ...), condition=%wide.region_2.3_spmd, body=%wide.region_1.2_spmd.sunk | while | flops 100360 | bytes 1706193 | solution.py:171
  181.2 3.7 %collective-permute-done.8 = bf16[1,32,256]{2,0,1:T(2,128)(2,1)S(1)} collective-permute-done((bf16[1,32,256]{2,0,1:T(2,128)(2,1)S(1)}, bf16[1,32,256]{2,0,1:T(2,128)(2,1)S(1)}, u32[]{:S(2)}, u32[]{:S(2)}) %collective-permute-start.8) | collective-permute-done | bytes 16416 | tf_op jit(solution)/shard_map/ppermute | solution.py:41
  187.6 4.4 %collective-permute-done.10 = bf16[18,1,256]{2,0,1:T(8,128)(2,1)S(1)} collective-permute-done((bf16[18,1,256]{2,0,1:T(8,128)(2,1)S(1)}, bf16[18,1,256]{2,0,1:T(8,128)(2,1)S(1)}, u32[]{:S(2)}, u32[]{:S(2)}) %collective-permute-start.10) | collective-permute-done | bytes 9248 | tf_op jit(solution)/shard_map/ppermute | solution.py:41
  194.3 79.8 %all-reduce.5.cloned.1.call-done = (f32[3,3,256,256]{3,2,1,0:T(8,128)}, f32[3,3,256,256]{3,2,1,0:T(8,128)}) async-done(((f32[3,3,256,256]{3,2,1,0:T(8,128)}, f32[3,3,256,256]{3,2,1,0:T(8,128)}), (f32[3,3,256,256]{3,2,1,0:T(8,128)}, f32[3,3,256,256]{3,2,1,0:T(8,128)})) %all-reduce.5.cloned.1.call-update) | async-done | bytes 4718608 | tf_op jit(solution)/shard_map/psum | solution.py:159
  274.1 3.4 %broadcast_multiply_fusion.1 = f32[3,3,256,256]{3,2,1,0:T(8,128)} fusion(f32[3,3,256,256]{3,2,1,0:T(8,128)} %get-tuple-element.153), kind=kLoop, calls=%fused_computation.30 | loop fusion | flops 589824 | bytes 4718592 | tf_op jit(solution)/shard_map/mul | solution.py:177
  277.5 1.6 broadcast_multiply_fusion
  (227 shorter events, 85.9 us)
Async XLA Ops:
  7.2 49.5 %copy-start = (bf16[3,3,256,256]{3,2,1,0:T(8,128)(2,1)S(1)}, bf16[3,3,256,256]{3,2,1,0:T(8,128)(2,1)}, u32[]{:S(2)}) copy-start(bf16[3,3,256,256]{3,2,1,0:T(8,128)(2,1)} %param.11) | copy-start | bytes 3538948
  11.7 67.8 %all-to-all-start = ((bf16[4,2,4]{2,1,0:T(2,128)(2,1)}), bf16[4,2,4]{2,1,0:T(2,128)(2,1)S(1)}, u32[]{:S(2)}, u32[]{:S(2)}) async-start(bf16[4,2,4]{2,1,0:T(2,128)(2,1)} %bitcast.9), calls=%async_computation | async-start | bytes 4096 | tf_op jit(solution)/shard_map/all_to_all | solution.py:133
  18.8 6.1 %collective-permute-start.1 = (bf16[1,32,256]{2,1,0:T(8,128)(2,1)S(1)}, bf16[1,32,256]{2,1,0:T(8,128)(2,1)S(1)}, u32[]{:S(2)}, u32[]{:S(2)}) collective-permute-start(bf16[1,32,256]{2,1,0:T(8,128)(2,1)S(1)} %get-tuple-element.177), channel_id=1, source_target_pairs={{4,0},{8,4},{12,8},{16,12},{20,16},{24,20},{28,24},{5,1},{9,5},{13... | collective-permute-start | bytes 49160 | tf_op jit(solution)/shard_map/ppermute | solution.py:41
  20.1 3.9 %collective-permute-start = (bf16[1,32,256]{2,1,0:T(8,128)(2,1)S(1)}, bf16[1,32,256]{2,1,0:T(8,128)(2,1)S(1)}, u32[]{:S(2)}, u32[]{:S(2)}) collective-permute-start(bf16[1,32,256]{2,1,0:T(8,128)(2,1)S(1)} %get-tuple-element.178), channel_id=1, source_target_pairs={{0,4},{4,8},{8,12},{12,16},{16,20},{20,24},{24,28},{1,5},{5,9},{9,... | collective-permute-start | bytes 49160 | tf_op jit(solution)/shard_map/ppermute | solution.py:40
  25.0 5.4 %collective-permute-start.2 = (bf16[18,1,256]{2,1,0:T(2,128)(2,1)S(1)}, bf16[18,1,256]{2,1,0:T(2,128)(2,1)S(1)}, u32[]{:S(2)}, u32[]{:S(2)}) collective-permute-start(bf16[18,1,256]{2,1,0:T(2,128)(2,1)S(1)} %get-tuple-element.173), channel_id=1, source_target_pairs={{0,1},{1,2},{2,3},{4,5},{5,6},{6,7},{8,9},{9,10},{10,11},{12,13},{... | collective-permute-start | bytes 27656 | tf_op jit(solution)/shard_map/ppermute | solution.py:40
  28.9 5.7 %collective-permute-start.3 = (bf16[18,1,256]{2,1,0:T(2,128)(2,1)S(1)}, bf16[18,1,256]{2,1,0:T(2,128)(2,1)S(1)}, u32[]{:S(2)}, u32[]{:S(2)}) collective-permute-start(bf16[18,1,256]{2,1,0:T(2,128)(2,1)S(1)} %get-tuple-element.174), channel_id=1, source_target_pairs={{1,0},{2,1},{3,2},{5,4},{6,5},{7,6},{9,8},{10,9},{11,10},{13,12},{... | collective-permute-start | bytes 27656 | tf_op jit(solution)/shard_map/ppermute | solution.py:41
  51.9 4.8 %copy-start.19 = (pred[8,5]{0,1:T(8,128)(4,1)S(1)}, pred[8,5]{0,1:T(8,128)(4,1)}, u32[]{:S(2)}) copy-start(pred[8,5]{0,1:T(8,128)(4,1)} %constant.160) | copy-start | bytes 124
  52.2 8.3 %collective-permute-start.6 = (bf16[1,2,16,16,256]{4,3,2,1,0:T(8,128)(2,1)S(1)}, bf16[1,2,16,16,256]{4,3,2,1,0:T(8,128)(2,1)S(1)}, u32[]{:S(2)}, u32[]{:S(2)}) collective-permute-start(bf16[1,2,16,16,256]{4,3,2,1,0:T(8,128)(2,1)S(1)} %get-tuple-element.160), channel_id=1, source_target_pairs={{0,3},{1,0},{2,1},{3,2},{4,7},{5,4},{6,5},{7,6},{8,11},{9,8},{10,9... | collective-permute-start | bytes 786440 | tf_op jit(solution)/shard_map/ppermute | solution.py:28
  53.7 24.5 %collective-permute-start.5 = (bf16[1,2,16,16,256]{4,3,2,1,0:T(8,128)(2,1)S(1)}, bf16[1,2,16,16,256]{4,3,2,1,0:T(8,128)(2,1)S(1)}, u32[]{:S(2)}, u32[]{:S(2)}) collective-permute-start(bf16[1,2,16,16,256]{4,3,2,1,0:T(8,128)(2,1)S(1)} %get-tuple-element.161), channel_id=1, source_target_pairs={{0,2},{1,3},{2,0},{3,1},{4,6},{5,7},{6,4},{7,5},{8,10},{9,11},{10,... | collective-permute-start | bytes 786440 | tf_op jit(solution)/shard_map/ppermute | solution.py:28
  55.2 23.0 %collective-permute-start.4 = (bf16[1,2,16,16,256]{4,3,2,1,0:T(8,128)(2,1)S(1)}, bf16[1,2,16,16,256]{4,3,2,1,0:T(8,128)(2,1)S(1)}, u32[]{:S(2)}, u32[]{:S(2)}) collective-permute-start(bf16[1,2,16,16,256]{4,3,2,1,0:T(8,128)(2,1)S(1)} %get-tuple-element.162), channel_id=1, source_target_pairs={{0,1},{1,2},{2,3},{3,0},{4,5},{5,6},{6,7},{7,4},{8,9},{9,10},{10,1... | collective-permute-start | bytes 786440 | tf_op jit(solution)/shard_map/ppermute | solution.py:28
  84.4 1.8 copy-start.17
  95.0 6.2 %copy-start.4 = (bf16[14,4,16,256]{3,2,1,0:T(8,128)(2,1)}, bf16[14,4,16,256]{3,2,1,0:T(8,128)(2,1)S(1)}, u32[]{:S(2)}) copy-start(bf16[14,4,16,256]{3,2,1,0:T(8,128)(2,1)S(1)} %reshape.200) | copy-start | bytes 1376260
  106.1 5.3 %copy-start.10 = (bf16[4,14,14,256]{3,2,1,0:T(8,128)(2,1)S(1)}, bf16[4,14,14,256]{3,2,1,0:T(8,128)(2,1)}, u32[]{:S(2)}) copy-start(bf16[4,14,14,256]{3,2,1,0:T(8,128)(2,1)} %copy_bitcast_fusion.2) | copy-start | bytes 1204228
  107.8 23.5 %all-to-all-start.1 = ((bf16[4,2,14,14,256]{4,1,3,2,0:T(2,128)(2,1)}), bf16[4,2,14,14,256]{4,1,3,2,0:T(2,128)(2,1)S(1)}, u32[]{:S(2)}, u32[]{:S(2)}) async-start(bf16[4,2,14,14,256]{4,1,3,2,0:T(2,128)(2,1)} %copy.105), calls=%async_computation.1 | async-start | bytes 1605632 | tf_op jit(solution)/shard_map/all_to_all | solution.py:154
  111.3 1.5 copy-start.12
  111.3 162.8 %all-reduce.5.cloned.1.call-start = ((), (), s32[]{:S(2)}) async-start(), calls=%async_computation.2 | async-start | bytes 9437184 | tf_op jit(solution)/shard_map/psum | solution.py:159
  123.7 1.5 copy-start.2
  131.5 1.3 copy-start.15
  132.8 45.5 %copy-start.3 = (f32[16,8,5,256]{3,0,2,1:T(8,128)S(1)}, f32[16,8,5,256]{3,0,2,1:T(8,128)}, u32[]{:S(2)}) copy-start(f32[16,8,5,256]{3,0,2,1:T(8,128)} %copy.111) | copy-start | bytes 1966084
  178.6 2.6 collective-permute-start.7
  179.9 5.0 %collective-permute-start.8 = (bf16[1,32,256]{2,0,1:T(2,128)(2,1)S(1)}, bf16[1,32,256]{2,0,1:T(2,128)(2,1)S(1)}, u32[]{:S(2)}, u32[]{:S(2)}) collective-permute-start(bf16[1,32,256]{2,0,1:T(2,128)(2,1)S(1)} %get-tuple-element.176), channel_id=1, source_target_pairs={{4,0},{8,4},{12,8},{16,12},{20,16},{24,20},{28,24},{5,1},{9,5},{13... | collective-permute-start | bytes 49160 | tf_op jit(solution)/shard_map/ppermute | solution.py:41
  184.9 2.7 collective-permute-start.9
  186.2 5.8 %collective-permute-start.10 = (bf16[18,1,256]{2,0,1:T(8,128)(2,1)S(1)}, bf16[18,1,256]{2,0,1:T(8,128)(2,1)S(1)}, u32[]{:S(2)}, u32[]{:S(2)}) collective-permute-start(bf16[18,1,256]{2,0,1:T(8,128)(2,1)S(1)} %get-tuple-element.172), channel_id=1, source_target_pairs={{1,0},{2,1},{3,2},{5,4},{6,5},{7,6},{9,8},{10,9},{11,10},{13,12},{... | collective-permute-start | bytes 27656 | tf_op jit(solution)/shard_map/ppermute | solution.py:41
  274.1 3.4 %copy-start.1 = (f32[3,3,256,256]{3,2,1,0:T(8,128)S(1)}, f32[3,3,256,256]{3,2,1,0:T(8,128)}, u32[]{:S(2)}) copy-start(f32[3,3,256,256]{3,2,1,0:T(8,128)} %get-tuple-element.154) | copy-start | bytes 7077892
  (10 other events, 10.4 us)
Sparse Core Ops, SparseCore 0:
  128.5 145.5 all-reduce.4
